TPU v7x, 512 devices: a whole 4x4x16 slice. The times are simulated.
512 devices in a mesh: ctx: 32 (over x, z_lo, core), tp: 16 (over y, z_hi).
Axes of the slice: x: 4, y: 4, z: 16 (z_hi: 4, z_lo: 4; z = z_hi * 4 + z_lo), core: 2. Of those that a mesh axis runs over, the one named last changes fastest.
Arguments:
- attention_out: bfloat16 [512, 8192], P('ctx', 'tp'), may hold values from -6 to 6
- w_out: bfloat16 [8192, 8192], P('tp', 'ctx'), may hold values from -0.0625 to 0.0625
- residual: bfloat16 [512, 8192], P(('ctx', 'tp')), may hold values from -6 to 6
- norm_gain: float32 [8192], replicated, may hold values from 0.1 to 1.9
- w_gate: bfloat16 [28672, 8192], P(('ctx', 'tp')), may hold values from -0.0625 to 0.0625
- w_up: bfloat16 [28672, 8192], P(('ctx', 'tp')), may hold values from -0.0625 to 0.0625
- w_down: bfloat16 [32, 896, 8192], P(None, 'tp', 'ctx'), may hold values from -0.03125 to 0.03125
Outputs:
- mixed: bfloat16 [512, 8192], P(('ctx', 'tp'))
All inputs are finite; a program needn't handle non-finite values.
Results may differ from a plain program's by a relative error of at most 0.02.
Values may be sent and summed in bfloat16 or wider, within the bound.
No kernel may reach another device: no remote copies, remote signals or barrier semaphores. Data moves between devices by JAX's collectives and lax.ppermute only.
A program may use at most 64 MiB of HBM per device.

v0:
```python
import jax
import jax.numpy as jnp
from jax import lax
from jax.sharding import PartitionSpec as P


def owner_order(partial_value, ctx_count, tp_count, row_count):
    col_count = partial_value.shape[1]
    grouped = partial_value.reshape(ctx_count, tp_count, row_count, col_count)
    return jnp.transpose(grouped, (1, 0, 2, 3)).reshape(tp_count * ctx_count * row_count, col_count)


def shards(attention_out, w_out, residual, norm_gain, w_gate, w_up, w_down):
    row_count = residual.shape[0]
    ctx_count = lax.axis_size("ctx")
    tp_count = lax.axis_size("tp")
    unit_count = w_gate.shape[0]
    col_count = w_down.shape[2]
    partial_value = jnp.dot(
        lax.all_gather(attention_out, "ctx", axis=0, tiled=True),
        w_out,
        preferred_element_type=jnp.float32,
    )
    summed = lax.psum_scatter(
        owner_order(partial_value, ctx_count, tp_count, row_count).astype(jnp.bfloat16),
        "tp",
        scatter_dimension=0,
        tiled=True,
    ).astype(jnp.float32)
    proj = lax.all_to_all(
        summed.astype(jnp.bfloat16), "ctx", split_axis=0, concat_axis=1, tiled=True
    ).astype(summed.dtype)
    carried = residual.astype(jnp.float32) + proj
    mean_square = jnp.mean(carried * carried, axis=-1, keepdims=True)
    normed = (carried * lax.rsqrt(mean_square + 1e-05) * norm_gain).astype(jnp.bfloat16)
    paired = jnp.concatenate([w_gate, w_up], axis=0)
    group = lax.all_gather(normed, "tp", axis=0, tiled=True)
    gate_up = lax.dot_general(
        lax.all_gather(group, "ctx", axis=0, tiled=True),
        paired,
        (((1,), (1,)), ((), ())),
        preferred_element_type=jnp.float32,
    )
    gate_part = gate_up[:, :unit_count]
    up_part = gate_up[:, unit_count:]
    hidden = (jax.nn.silu(gate_part) * up_part).astype(jnp.bfloat16)
    flat_down = w_down.reshape(ctx_count * unit_count, col_count)
    partial_down = jnp.dot(
        lax.all_gather(hidden, "ctx", axis=1, tiled=True),
        flat_down,
        preferred_element_type=jnp.float32,
    )
    reduced = lax.psum_scatter(
        owner_order(partial_down, ctx_count, tp_count, row_count).astype(jnp.bfloat16),
        "tp",
        scatter_dimension=0,
        tiled=True,
    ).astype(jnp.float32)
    down = lax.all_to_all(
        reduced.astype(jnp.bfloat16), "ctx", split_axis=0, concat_axis=1, tiled=True
    ).astype(reduced.dtype)
    return (carried + down).astype(jnp.bfloat16)


def solution(mesh):
    in_specs = (
        P("ctx", "tp"),
        P("tp", "ctx"),
        P(("ctx", "tp"), None),
        P(),
        P(("ctx", "tp"), None),
        P(("ctx", "tp"), None),
        P(None, "tp", "ctx"),
    )
    out_specs = P(("ctx", "tp"), None)
    return jax.shard_map(shards, mesh=mesh, in_specs=in_specs, out_specs=out_specs, check_vma=False)
```

profile of v0, /device:TPU:1, one launch (start us, length us, event | category | flops | bytes accessed | tf_op | source)
XLA Modules:
  0.0 513.3 jit_solution(6987445112993718375)
XLA Ops:
  6.5 0.0 copy-start
  6.5 0.0 copy-start.1
  6.5 0.0 copy-start.2
  6.5 0.0 reduce-scatter.3.cloned.1.call-start
  6.5 48.2 %all_gather.12 = bf16[512,512]{1,0:T(8,128)(2,1)S(1)} all-gather(bf16[16,512]{1,0:T(8,128)(2,1)} %param.7), channel_id=1, replica_groups=mesh['ctx'=32,'tp'=16] {'ctx'}, dimensions={0}, use_global_device_ids=true | all-gather | bytes 540672 | tf_op jit(solution)/shard_map/all_gather | solution.py:20
  54.7 0.0 copy-start.3
  54.7 0.0 copy-start.4
  54.7 1.4 convolution_convert_fusion.1
  56.1 0.8 copy.12
  56.9 0.0 reduce-scatter.3.cloned.1.call-update
  56.9 0.0 all-gather.4.cloned.1.call-start
  56.9 108.8 %reduce-scatter.3.cloned.1.call-done = bf16[32,256]{1,0:T(8,128)(2,1)} async-done(((bf16[512,256]{1,0:T(8,128)(2,1)}), bf16[32,256]{1,0:T(8,128)(2,1)}) %reduce-scatter.3.cloned.1.call-update) | async-done | bytes 16400 | tf_op jit(solution)/shard_map/reduce_scatter | solution.py:24
  165.8 0.5 broadcast.4
  166.3 1.4 reduce.1
  167.6 14.4 %all_to_all.26 = bf16[32,2,128]{2,1,0:T(2,128)(2,1)S(1)} all-to-all(bf16[32,2,128]{2,1,0:T(2,128)(2,1)S(1)} %reshape.72), channel_id=1, replica_groups=mesh['ctx'=32,'tp'=16] {'ctx'}, dimensions={0} | all-to-all | bytes 32768 | tf_op jit(solution)/shard_map/all_to_all | solution.py:30
  182.0 0.0 copy-done.1
  182.1 0.7 multiply_reduce_fusion
  183.5 0.0 copy-done.2
  183.5 0.1 convert_bitcast_fusion
  183.6 50.3 %all-gather = bf16[16,1,8192]{2,1,0:T(2,128)(2,1)S(1)} all-gather(bf16[1,1,8192]{2,1,0:T(2,128)(2,1)S(1)} %convert_bitcast_fusion), channel_id=1, replica_groups=mesh['ctx'=32,'tp'=16] {'tp'}, dimensions={0}, use_global_device_ids=true | all-gather | bytes 278528 | tf_op jit(solution)/shard_map/all_gather | solution.py:37
  233.9 1.0 copy.19
  234.9 0.0 all-gather.4.cloned.1.call-update
  234.9 0.0 all-gather.6.cloned.1.call-start
  235.0 71.6 %all-gather.4.cloned.1.call-done = bf16[512,8192]{1,0:T(8,128)(2,1)} async-done(((bf16[16,8192]{1,0:T(8,128)(2,1)}), bf16[512,8192]{1,0:T(8,128)(2,1)}) %all-gather.4.cloned.1.call-update) | async-done | bytes 8388624 | tf_op jit(solution)/shard_map/all_gather | solution.py:39
  306.5 0.0 copy-done.3
  306.5 0.0 copy-done.4
  306.5 6.2 %fusion = f32[512,112]{0,1:T(8,128)S(1)} fusion(bf16[512,8192]{1,0:T(8,128)(2,1)} %all-gather.4.cloned.1.call-done, bf16[56,8192]{1,0:T(8,128)(2,1)S(1)} %copy-done.3, bf16[56,8192]{1,0:T(8,128)(2,1)S(1)} %copy-done.4), kind=kOutput, calls=%fused_computation | convolution fusion | flops 943194112 | bytes 10452992 | tf_op jit(solution)/shard_map/dot_general | solution.py:38
  312.8 0.7 fusion.5
  313.4 0.0 all-gather.6.cloned.1.call-update
  313.5 0.0 reduce-scatter.5.cloned.1.call-start
  313.5 64.0 %all-gather.6.cloned.1.call-done = bf16[512,1792]{0,1:T(8,128)(2,1)} async-done(((bf16[512,56]{0,1:T(8,128)(2,1)}), bf16[512,1792]{0,1:T(8,128)(2,1)}) %all-gather.6.cloned.1.call-update) | async-done | bytes 1835024 | tf_op jit(solution)/shard_map/all_gather | solution.py:49
  377.5 2.8 copy.14
  380.3 0.0 copy-done
  380.3 0.6 fusion.4
  380.9 0.8 copy.15
  381.7 0.0 reduce-scatter.5.cloned.1.call-update
  381.7 108.5 %reduce-scatter.5.cloned.1.call-done = bf16[32,256]{1,0:T(8,128)(2,1)} async-done(((bf16[512,256]{1,0:T(8,128)(2,1)}), bf16[32,256]{1,0:T(8,128)(2,1)}) %reduce-scatter.5.cloned.1.call-update) | async-done | bytes 16400 | tf_op jit(solution)/shard_map/reduce_scatter | solution.py:53
  490.3 1.4 reduce.2
  491.6 14.4 %all_to_all.27 = bf16[32,2,128]{2,1,0:T(2,128)(2,1)S(1)} all-to-all(bf16[32,2,128]{2,1,0:T(2,128)(2,1)S(1)} %reshape.74), channel_id=1, replica_groups=mesh['ctx'=32,'tp'=16] {'ctx'}, dimensions={0} | all-to-all | bytes 32768 | tf_op jit(solution)/shard_map/all_to_all | solution.py:59
  506.1 0.7 fusion.6
  (4 shorter events, 0.1 us)
Async XLA Ops:
  6.5 373.7 %copy-start = (bf16[32,56,256]{2,1,0:T(8,128)(2,1)S(1)}, bf16[32,56,256]{2,1,0:T(8,128)(2,1)}, u32[]{:S(2)}) copy-start(bf16[32,56,256]{2,1,0:T(8,128)(2,1)} %param.13) | copy-start | bytes 2752516
  6.5 175.5 %copy-start.1 = (bf16[1,8192]{1,0:T(2,128)(2,1)S(1)}, bf16[1,8192]{1,0:T(2,128)(2,1)}, u32[]{:S(2)}) copy-start(bf16[1,8192]{1,0:T(2,128)(2,1)} %param.9) | copy-start | bytes 49156
  6.5 176.9 %copy-start.2 = (f32[8192]{0:T(1024)S(1)}, f32[8192]{0:T(1024)}, u32[]{:S(2)}) copy-start(f32[8192]{0:T(1024)} %param.10) | copy-start | bytes 98308
  6.5 159.2 %reduce-scatter.3.cloned.1.call-start = ((), (), s32[]{:S(2)}) async-start(), calls=%async_computation.4 | async-start | bytes 278528 | tf_op jit(solution)/shard_map/reduce_scatter | solution.py:24
  54.7 251.8 %copy-start.3 = (bf16[56,8192]{1,0:T(8,128)(2,1)S(1)}, bf16[56,8192]{1,0:T(8,128)(2,1)}, u32[]{:S(2)}) copy-start(bf16[56,8192]{1,0:T(8,128)(2,1)} %param.12) | copy-start | bytes 2752516
  54.7 251.8 %copy-start.4 = (bf16[56,8192]{1,0:T(8,128)(2,1)S(1)}, bf16[56,8192]{1,0:T(8,128)(2,1)}, u32[]{:S(2)}) copy-start(bf16[56,8192]{1,0:T(8,128)(2,1)} %param.11) | copy-start | bytes 2752516
  56.9 249.6 %all-gather.4.cloned.1.call-start = ((), (), s32[]{:S(2)}) async-start(), calls=%async_computation.5 | async-start | bytes 8650752 | tf_op jit(solution)/shard_map/all_gather | solution.py:39
  234.9 142.6 %all-gather.6.cloned.1.call-start = ((), (), s32[]{:S(2)}) async-start(), calls=%async_computation.6 | async-start | bytes 1892352 | tf_op jit(solution)/shard_map/all_gather | solution.py:49
  313.5 176.8 %reduce-scatter.5.cloned.1.call-start = ((), (), s32[]{:S(2)}) async-start(), calls=%async_computation.7 | async-start | bytes 278528 | tf_op jit(solution)/shard_map/reduce_scatter | solution.py:53
Sparse Core Ops, SparseCore 0:
  57.0 108.6 reduce-scatter.2
  235.0 71.4 all-gather.3
  313.6 63.8 all-gather.5
  381.9 108.2 reduce-scatter.4
where the time goes:
time: 514 us; the launch traced here: 513 us
  waiting for transfers between devices  353 us (69%)
  blocking collectives  127 us (25%)
  between operations  13.9 us (3%)
  matrix products  8.23 us (2%)
  local copies, waits for them, and re-layouts  5.9 us (1%)
    reduce_scatter x1, waiting for transfers between devices, shards(): lax.psum_scatter(owner_order(partial_value, ctx_count, tp_count, row_coun...  109 us
    reduce_scatter x1, waiting for transfers between devices, shards(): lax.psum_scatter(owner_order(partial_down, ctx_count, tp_count, row_count...  109 us
    all_gather x1, waiting for transfers between devices, shards(): lax.all_gather(group, 'ctx', axis=0, tiled=True)  71.6 us
    all_gather x1, waiting for transfers between devices, shards(): lax.all_gather(hidden, 'ctx', axis=1, tiled=True)  64 us
    all_gather x1, blocking collectives, shards(): group = lax.all_gather(normed, 'tp', axis=0, tiled=True)  50.3 us
    all_gather x1, blocking collectives, shards(): lax.all_gather(attention_out, 'ctx', axis=0, tiled=True)  48.2 us
    all_to_all x1, blocking collectives, shards(): lax.all_to_all(reduced.astype(jnp.bfloat16), 'ctx', split_axis=0, concat_...  14.4 us
    all_to_all x1, blocking collectives, shards(): lax.all_to_all(summed.astype(jnp.bfloat16), 'ctx', split_axis=0, concat_a...  14.4 us
  transfers between devices with their start and end apart: 4, of which 4 were waited for; matrix products, arithmetic and copies ran while one was open for 0% of the time, Pallas kernels for 0%

commit v1 on v0

--- a/solution.py
+++ b/solution.py
@@ -2,6 +2,13 @@
 import jax.numpy as jnp
 from jax import lax
 from jax.sharding import PartitionSpec as P
+
+
+def exchange_gather(x, axis, d):
+    size = lax.axis_size(axis)
+    blocks = jnp.stack([x for _ in range(size)])
+    blocks = lax.all_to_all(blocks, axis, split_axis=0, concat_axis=0)
+    return jnp.concatenate(blocks, axis=d)
 
 
 def owner_order(partial_value, ctx_count, tp_count, row_count):
@@ -46,9 +53,7 @@
     hidden = (jax.nn.silu(gate_part) * up_part).astype(jnp.bfloat16)
     flat_down = w_down.reshape(ctx_count * unit_count, col_count)
     partial_down = jnp.dot(
-        lax.all_gather(hidden, "ctx", axis=1, tiled=True),
-        flat_down,
-        preferred_element_type=jnp.float32,
+        exchange_gather(hidden, "ctx", 1), flat_down, preferred_element_type=jnp.float32
     )
     reduced = lax.psum_scatter(
         owner_order(partial_down, ctx_count, tp_count, row_count).astype(jnp.bfloat16),

time: 514 us -> 509 us (level)
  waiting for transfers between devices: 353 us -> 288 us
  blocking collectives: 127 us -> 178 us
  local copies, waits for them, and re-layouts: 5.9 us -> 16.9 us
    all_gather x1 -> x0, waiting for transfers between devices: 64 us -> none  [shards(): lax.all_gather(hidden, 'ctx', axis=1, tiled=True)]
    all_to_all x0 -> x1, blocking collectives: none -> 50.4 us  [exchange_gather(): blocks = lax.all_to_all(blocks, axis, split_axis=0, concat_axis=0)]
    dot_general x0 -> x1, local copies, waits for them, and re-layouts: none -> 7.03 us  [shards(): jnp.dot(exchange_gather(hidden, 'ctx', 1), flat_down, preferred_element_t...]
    reshape x0 -> x1, local copies, waits for them, and re-layouts: none -> 6.63 us  [exchange_gather(): return jnp.concatenate(blocks, axis=d)]
  transfers between devices with their start and end apart: 4 -> 3, of which waited for: 4 -> 3; matrix products, arithmetic and copies ran while one was open for 0% -> 0% of each run, Pallas kernels for 0% -> 0%
where the time goes in v1:
time: 509 us
  waiting for transfers between devices  288 us (57%)
  blocking collectives  178 us (35%)
  local copies, waits for them, and re-layouts  16.9 us (3%)
  between operations  13.9 us (3%)
  matrix products  8.23 us (2%)
    reduce_scatter x1, waiting for transfers between devices, shards(): lax.psum_scatter(owner_order(partial_value, ctx_count, tp_count, row_coun...  109 us
    reduce_scatter x1, waiting for transfers between devices, shards(): lax.psum_scatter(owner_order(partial_down, ctx_count, tp_count, row_count...  107 us
    all_gather x1, waiting for transfers between devices, shards(): lax.all_gather(group, 'ctx', axis=0, tiled=True)  71.6 us
    all_to_all x1, blocking collectives, exchange_gather(): blocks = lax.all_to_all(blocks, axis, split_axis=0, concat_axis=0)  50.4 us
    all_gather x1, blocking collectives, shards(): group = lax.all_gather(normed, 'tp', axis=0, tiled=True)  50.3 us
    all_gather x1, blocking collectives, shards(): lax.all_gather(attention_out, 'ctx', axis=0, tiled=True)  48.2 us
    all_to_all x1, blocking collectives, shards(): lax.all_to_all(reduced.astype(jnp.bfloat16), 'ctx', split_axis=0, concat_...  14.4 us
    all_to_all x1, blocking collectives, shards(): lax.all_to_all(summed.astype(jnp.bfloat16), 'ctx', split_axis=0, concat_a...  14.4 us
  transfers between devices with their start and end apart: 3, of which 3 were waited for; matrix products, arithmetic and copies ran while one was open for 0% of the time, Pallas kernels for 0%

profile of v1, /device:TPU:1, one launch (start us, length us, event | category | flops | bytes accessed | tf_op | source)
XLA Modules:
  0.0 508.8 jit_solution(4308372482130777843)
XLA Ops:
  6.5 0.0 copy-start
  6.5 0.0 copy-start.1
  6.5 0.0 copy-start.2
  6.5 0.0 reduce-scatter.3.cloned.1.call-start
  6.5 48.2 %all_gather.9 = bf16[512,512]{1,0:T(8,128)(2,1)S(1)} all-gather(bf16[16,512]{1,0:T(8,128)(2,1)} %param.7), channel_id=1, replica_groups=mesh['ctx'=32,'tp'=16] {'ctx'}, dimensions={0}, use_global_device_ids=true | all-gather | bytes 540672 | tf_op jit(solution)/shard_map/all_gather | solution.py:27
  54.7 0.0 copy-start.3
  54.7 0.0 copy-start.4
  54.7 1.4 convolution_convert_fusion.1
  56.1 0.8 copy.12
  56.9 0.0 reduce-scatter.3.cloned.1.call-update
  56.9 0.0 all-gather.3.cloned.1.call-start
  57.0 108.8 %reduce-scatter.3.cloned.1.call-done = bf16[32,256]{1,0:T(8,128)(2,1)} async-done(((bf16[512,256]{1,0:T(8,128)(2,1)}), bf16[32,256]{1,0:T(8,128)(2,1)}) %reduce-scatter.3.cloned.1.call-update) | async-done | bytes 16400 | tf_op jit(solution)/shard_map/reduce_scatter | solution.py:31
  165.8 0.5 broadcast.6
  166.3 1.4 reduce.1
  167.7 14.4 %all_to_all.31 = bf16[32,2,128]{2,1,0:T(2,128)(2,1)S(1)} all-to-all(bf16[32,2,128]{2,1,0:T(2,128)(2,1)S(1)} %reshape.80), channel_id=1, replica_groups=mesh['ctx'=32,'tp'=16] {'ctx'}, dimensions={0} | all-to-all | bytes 32768 | tf_op jit(solution)/shard_map/all_to_all | solution.py:37
  182.0 0.0 copy-done.1
  182.1 0.7 multiply_reduce_fusion
  183.5 0.0 copy-done.2
  183.6 0.1 convert_bitcast_fusion
  183.6 50.3 %all-gather = bf16[16,1,8192]{2,1,0:T(2,128)(2,1)S(1)} all-gather(bf16[1,1,8192]{2,1,0:T(2,128)(2,1)S(1)} %convert_bitcast_fusion), channel_id=1, replica_groups=mesh['ctx'=32,'tp'=16] {'tp'}, dimensions={0}, use_global_device_ids=true | all-gather | bytes 278528 | tf_op jit(solution)/shard_map/all_gather | solution.py:44
  234.0 1.0 copy.19
  235.0 0.0 all-gather.3.cloned.1.call-update
  235.0 0.0 reduce-scatter.5.cloned.1.call-start
  235.0 71.6 %all-gather.3.cloned.1.call-done = bf16[512,8192]{1,0:T(8,128)(2,1)} async-done(((bf16[16,8192]{1,0:T(8,128)(2,1)}), bf16[512,8192]{1,0:T(8,128)(2,1)}) %all-gather.3.cloned.1.call-update) | async-done | bytes 8388624 | tf_op jit(solution)/shard_map/all_gather | solution.py:46
  306.6 0.0 copy-done.3
  306.6 0.0 copy-done.4
  306.6 6.2 %fusion = f32[512,112]{0,1:T(8,128)S(1)} fusion(bf16[512,8192]{1,0:T(8,128)(2,1)} %all-gather.3.cloned.1.call-done, bf16[56,8192]{1,0:T(8,128)(2,1)S(1)} %copy-done.3, bf16[56,8192]{1,0:T(8,128)(2,1)S(1)} %copy-done.4), kind=kOutput, calls=%fused_computation | convolution fusion | flops 943194112 | bytes 10452992 | tf_op jit(solution)/shard_map/dot_general | solution.py:45
  312.9 0.1 stack.2
  313.0 50.4 %all_to_all.32 = bf16[32,512,56]{1,2,0:T(8,128)(2,1)S(1)} all-to-all(bf16[32,512,56]{1,2,0:T(8,128)(2,1)S(1)} %stack.2), channel_id=1, replica_groups=mesh['ctx'=32,'tp'=16] {'ctx'}, dimensions={0} | all-to-all | bytes 3670016 | tf_op jit(solution)/shard_map/all_to_all | solution.py:10
  363.4 6.6 %copy.14 = bf16[512,32,56]{2,1,0:T(8,128)(2,1)} copy(bf16[512,32,56]{0,2,1:T(8,128)(2,1)S(1)} %bitcast.31) | data formatting | bytes 3670016 | tf_op jit(solution)/shard_map/reshape | solution.py:11
  370.0 7.0 %dot_general.13 = bf16[32,16,1792]{2,1,0:T(8,128)(2,1)S(1)} reshape(bf16[512,32,56]{2,1,0:T(8,128)(2,1)} %copy.14) | data formatting | bytes 3670016 | tf_op jit(solution)/shard_map/dot_general | solution.py:55
  377.1 0.0 copy-done
  377.1 0.6 fusion.4
  377.7 0.8 copy.15
  378.5 0.0 reduce-scatter.5.cloned.1.call-update
  378.5 107.3 %reduce-scatter.5.cloned.1.call-done = bf16[32,256]{1,0:T(8,128)(2,1)} async-done(((bf16[512,256]{1,0:T(8,128)(2,1)}), bf16[32,256]{1,0:T(8,128)(2,1)}) %reduce-scatter.5.cloned.1.call-update) | async-done | bytes 16400 | tf_op jit(solution)/shard_map/reduce_scatter | solution.py:58
  485.8 1.4 reduce.2
  487.2 14.4 %all_to_all.33 = bf16[32,2,128]{2,1,0:T(2,128)(2,1)S(1)} all-to-all(bf16[32,2,128]{2,1,0:T(2,128)(2,1)S(1)} %reshape.82), channel_id=1, replica_groups=mesh['ctx'=32,'tp'=16] {'ctx'}, dimensions={0} | all-to-all | bytes 32768 | tf_op jit(solution)/shard_map/all_to_all | solution.py:64
  501.6 0.7 fusion.6
  (5 shorter events, 0.1 us)
Async XLA Ops:
  6.5 370.5 %copy-start = (bf16[32,56,256]{2,1,0:T(8,128)(2,1)S(1)}, bf16[32,56,256]{2,1,0:T(8,128)(2,1)}, u32[]{:S(2)}) copy-start(bf16[32,56,256]{2,1,0:T(8,128)(2,1)} %param.13) | copy-start | bytes 2752516
  6.5 175.5 %copy-start.1 = (bf16[1,8192]{1,0:T(2,128)(2,1)S(1)}, bf16[1,8192]{1,0:T(2,128)(2,1)}, u32[]{:S(2)}) copy-start(bf16[1,8192]{1,0:T(2,128)(2,1)} %param.9) | copy-start | bytes 49156
  6.5 177.0 %copy-start.2 = (f32[8192]{0:T(1024)S(1)}, f32[8192]{0:T(1024)}, u32[]{:S(2)}) copy-start(f32[8192]{0:T(1024)} %param.10) | copy-start | bytes 98308
  6.5 159.2 %reduce-scatter.3.cloned.1.call-start = ((), (), s32[]{:S(2)}) async-start(), calls=%async_computation.5 | async-start | bytes 278528 | tf_op jit(solution)/shard_map/reduce_scatter | solution.py:31
  54.7 251.9 %copy-start.3 = (bf16[56,8192]{1,0:T(8,128)(2,1)S(1)}, bf16[56,8192]{1,0:T(8,128)(2,1)}, u32[]{:S(2)}) copy-start(bf16[56,8192]{1,0:T(8,128)(2,1)} %param.12) | copy-start | bytes 2752516
  54.7 251.9 %copy-start.4 = (bf16[56,8192]{1,0:T(8,128)(2,1)S(1)}, bf16[56,8192]{1,0:T(8,128)(2,1)}, u32[]{:S(2)}) copy-start(bf16[56,8192]{1,0:T(8,128)(2,1)} %param.11) | copy-start | bytes 2752516
  56.9 249.7 %all-gather.3.cloned.1.call-start = ((), (), s32[]{:S(2)}) async-start(), calls=%async_computation.6 | async-start | bytes 8650752 | tf_op jit(solution)/shard_map/all_gather | solution.py:46
  235.0 250.8 %reduce-scatter.5.cloned.1.call-start = ((), (), s32[]{:S(2)}) async-start(), calls=%async_computation.7 | async-start | bytes 278528 | tf_op jit(solution)/shard_map/reduce_scatter | solution.py:58
Sparse Core Ops, SparseCore 0:
  57.0 108.6 reduce-scatter.2
  235.1 71.4 all-gather.2
  378.6 107.1 reduce-scatter.4
